TPU v7x, 256 devices: a whole 4x4x8 slice. The times are simulated.
256 devices in a mesh: dp: 8 (over z), expert: 32 (over x, y, core).
Axes of the slice: x: 4, y: 4, z: 8, core: 2. Of those that a mesh axis runs over, the one named last changes fastest.
Arguments:
- tokens: bfloat16 [32768, 7168], P(('dp', 'expert')), may hold values from -8 to 8
- routes: int32 [32768, 8], P(('dp', 'expert')), may hold values from 0 to 255, as said below
- slots: int32 [32768, 8], P(('dp', 'expert')), may hold values from 0 to 127, as said below
- gate_weight: bfloat16 [7168, 8192], P(None, 'expert'), may hold values from -0.0625 to 0.0625
- up_weight: bfloat16 [7168, 8192], P(None, 'expert'), may hold values from -0.0625 to 0.0625
Outputs:
- means: float32 [8192], P('expert')
- covariance: float32 [8192, 2048], P('expert', 'dp')
Inputs may be any that keep to these rules, and one draw needn't show every extreme that they name: `routes`: each row names 8 different experts; every row names expert 256 - 1. slots[t, k] is the number of earlier tokens of the same device (the rows of one device, 128 in a row) whose routes name routes[t, k]. Every expert below 4 fills all 16 of its slots from every device of at least one dp index.
All inputs are finite; a program needn't handle non-finite values.
Results may differ from a plain program's by a relative error of at most 0.0031.
Values may be sent and summed in bfloat16 or wider, within the bound.
A program may use at most 64 MiB of HBM per device.

v0:
```python
import jax
import jax.numpy as jnp
from jax import lax
from jax.sharding import PartitionSpec as P

FF = 2048
CAP = 16


def swapped(array, axis, stride):
    return lax.ppermute(array, axis, [(i, i ^ 1 << stride) for i in range(lax.axis_size(axis))])


def member_fan(current, upper_half, partner):
    leading = jnp.where(upper_half, partner, current)
    trailing = jnp.where(upper_half, current, partner)
    return jnp.concatenate([leading, trailing], axis=0)


def local(tokens, routes, slots, gate_weight, up_weight):
    tok_rows, features = tokens.shape
    hidden_units = gate_weight.shape[1]
    senders = lax.axis_size("expert")
    group_size = FF // hidden_units
    levels = group_size.bit_length() - 1
    experts = senders // group_size
    member = lax.axis_index("expert")
    owner_id = member // group_size
    offset = member % group_size
    usable = (routes < experts) & (slots < CAP)
    target = jnp.where(usable, routes * CAP + slots, -1)
    places = lax.broadcasted_iota(jnp.int32, (experts * CAP, tok_rows, routes.shape[1]), 0)
    placing = jnp.any(places == target[None], axis=2)
    packed = jnp.dot(
        placing.astype(jnp.bfloat16), tokens, preferred_element_type=jnp.float32
    ).astype(jnp.bfloat16)
    local_counts = jnp.sum(placing.astype(jnp.float32), axis=1).reshape(experts, CAP).sum(axis=1)
    outgoing = jnp.broadcast_to(
        packed.reshape(experts, 1, CAP, features), (experts, group_size, CAP, features)
    )
    outgoing = outgoing.reshape(senders, CAP, features)
    arrived = lax.all_to_all(outgoing, "expert", split_axis=0, concat_axis=0, tiled=True)
    gate_sums = jnp.einsum("scd,du->scu", arrived, gate_weight, preferred_element_type=jnp.float32)
    up_sums = jnp.einsum("scd,du->scu", arrived, up_weight, preferred_element_type=jnp.float32)
    hidden = (jax.nn.silu(gate_sums) * up_sums).astype(jnp.bfloat16)
    hidden = hidden.reshape(senders * CAP, hidden_units)
    stacked = hidden[None]
    for bit_level in range(levels):
        partner = swapped(stacked, "expert", bit_level)
        stacked = member_fan(stacked, member >> bit_level & 1 == 1, partner)
    gram_block = jnp.einsum(
        "rj,krc->jkc", hidden, stacked, preferred_element_type=jnp.float32
    ).reshape(hidden_units, FF)
    column_sums = jnp.sum(stacked, axis=1, dtype=jnp.float32).reshape(FF)
    replicas = lax.axis_size("dp")
    share_cols = FF // replicas
    column_start = lax.axis_index("dp") * share_cols
    totals = lax.psum(local_counts, ("dp", "expert"))
    row_total = lax.dynamic_index_in_dim(totals, owner_id, 0, keepdims=False)
    merged, summed = lax.psum((gram_block, column_sums), "dp")
    cov_block = lax.dynamic_slice_in_dim(merged, column_start, share_cols, 1)
    means_all = summed / row_total
    row_means = lax.dynamic_slice_in_dim(means_all, offset * hidden_units, hidden_units, 0)
    column_means = lax.dynamic_slice_in_dim(means_all, column_start, share_cols, 0)
    covariance = cov_block / row_total - row_means[:, None] * column_means[None, :]
    return (row_means, covariance)


def solution(mesh):
    in_specs = (
        P(("dp", "expert"), None),
        P(("dp", "expert"), None),
        P(("dp", "expert"), None),
        P(None, "expert"),
        P(None, "expert"),
    )
    out_specs = (P("expert"), P("expert", "dp"))
    return jax.shard_map(local, mesh=mesh, in_specs=in_specs, out_specs=out_specs, check_vma=False)
```

profile of v0, /device:TPU:9, one launch (start us, length us, event | category | flops | bytes accessed | tf_op | source)
XLA Modules:
  0.0 255.0 jit_solution(1822630082755510537)
XLA Ops:
  7.2 0.0 copy-start
  7.2 0.0 all-reduce.2.cloned.1.call-start
  7.2 0.8 add_select_fusion
  8.1 0.1 fusion.10
  8.2 0.6 copy-done
  8.7 0.4 convolution_convert_fusion
  9.1 0.9 broadcast_in_dim.16
  10.0 0.0 copy-start.6
  10.0 90.3 %all_to_all.5 = bf16[32,16,7168]{2,1,0:T(8,128)(2,1)S(1)} all-to-all(bf16[32,16,7168]{2,1,0:T(8,128)(2,1)S(1)} %bitcast.26), channel_id=1, replica_groups=mesh['dp'=8,'expert'=32] {'expert'}, dimensions={0} | all-to-all | bytes 14680064 | tf_op jit(solution)/shard_map/all_to_all | solution.py:42
  100.4 0.0 copy-done.6
  100.4 0.0 copy-start.7
  100.4 2.1 fusion.2
  102.4 0.0 copy-done.7
  102.4 2.1 fusion.7
  104.6 0.0 copy-start.3
  104.6 0.1 copy.12
  104.7 1.0 collective-permute-start
  105.7 0.0 copy-done.3
  105.7 1.2 collective-permute-done
  106.9 0.1 pad_maximum_fusion.2
  107.0 1.5 collective-permute-start.1
  108.5 11.7 %collective-permute-done.1 = bf16[2,512,256]{1,2,0:T(8,128)(2,1)S(1)} collective-permute-done((bf16[2,512,256]{1,2,0:T(8,128)(2,1)S(1)}, bf16[2,512,256]{1,2,0:T(8,128)(2,1)S(1)}, u32[]{:S(2)}, u32[]{:S(2)}) %collective-permute-start.1) | collective-permute-done | bytes 524320 | tf_op jit(solution)/shard_map/ppermute | solution.py:11
  120.2 0.1 broadcast_select_fusion.3
  120.3 0.0 copy-start.2
  120.3 0.8 copy-done.2
  121.1 0.1 pad_maximum_fusion.1
  121.2 2.1 collective-permute-start.2
  123.3 23.1 %collective-permute-done.2 = bf16[4,512,256]{1,2,0:T(8,128)(2,1)} collective-permute-done((bf16[4,512,256]{1,2,0:T(8,128)(2,1)S(1)}, bf16[4,512,256]{1,2,0:T(8,128)(2,1)}, u32[]{:S(2)}, u32[]{:S(2)}) %collective-permute-start.2) | collective-permute-done | bytes 1048608 | tf_op jit(solution)/shard_map/ppermute | solution.py:11
  146.4 1.5 broadcast_select_fusion.1
  147.9 0.0 copy-start.1
  147.9 0.0 copy-start.4
  147.9 0.2 pad_maximum_fusion
  148.1 0.8 copy-done.1
  148.8 0.2 copy-done.4
  149.0 2.1 fusion.12
  151.1 0.0 all-reduce.2.cloned.1.call-update
  151.1 0.1 convert_reduce_fusion.1
  151.2 0.1 reshape.25
  151.3 0.1 reduce_sum.29
  151.4 79.7 %psum.22 = f32[4]{0:T(128)S(1)} all-reduce(f32[4]{0:T(128)S(1)} %reduce_sum.29), channel_id=1, replica_groups=mesh['dp'=8,'expert'=32] {'dp','expert'}, use_global_device_ids=true, to_apply=%region_5.6 | all-reduce | flops 4 | bytes 32 | tf_op jit(solution)/shard_map/psum | solution.py:58
  231.1 0.6 dynamic_slice.13
  231.7 1.6 convert_reduce_fusion
  233.3 11.7 %psum.21 = f32[2048]{0:T(1024)S(1)} all-reduce(f32[2048]{0:T(1024)S(1)} %bitcast.32), channel_id=1, replica_groups=mesh['dp'=8,'expert'=32] {'dp'}, use_global_device_ids=true, to_apply=%region_2.3 | all-reduce | flops 2048 | bytes 16384 | tf_op jit(solution)/shard_map/psum | solution.py:60
  245.0 0.6 broadcast_divide_fusion
  245.7 0.1 fusion.11
  245.7 0.0 copy-start.5
  245.7 0.0 all-reduce.2.cloned.1.call-done
  245.7 2.4 multiply_subtract_fusion
  248.1 0.0 copy-done.5
  (2 shorter events, 0.0 us)
Async XLA Ops:
  7.2 1.5 copy-start
  7.2 238.6 %all-reduce.2.cloned.1.call-start = ((), (), s32[]{:S(2)}) async-start(), calls=%async_computation.1 | async-start | bytes 4194304 | tf_op jit(solution)/shard_map/psum | solution.py:60
  10.0 90.3 %copy-start.6 = (bf16[7168,256]{1,0:T(8,128)(2,1)S(1)}, bf16[7168,256]{1,0:T(8,128)(2,1)}, u32[]{:S(2)}) copy-start(bf16[7168,256]{1,0:T(8,128)(2,1)} %param.8) | copy-start | bytes 11010052
  100.4 2.1 copy-start.7
  104.6 1.2 copy-start.3
  104.7 2.2 collective-permute-start
  107.0 13.2 %collective-permute-start.1 = (bf16[2,512,256]{1,2,0:T(8,128)(2,1)S(1)}, bf16[2,512,256]{1,2,0:T(8,128)(2,1)S(1)}, u32[]{:S(2)}, u32[]{:S(2)}) collective-permute-start(bf16[2,512,256]{1,2,0:T(8,128)(2,1)S(1)} %pad_maximum_fusion.2), channel_id=1, source_target_pairs={{0,2},{1,3},{2,0},{3,1},{4,6},{5,7},{6,4},{7,5},{8,10},{9,11},{10,... | collective-permute-start | bytes 1572872 | tf_op jit(solution)/shard_map/ppermute | solution.py:11
  120.3 0.8 copy-start.2
  121.2 25.1 %collective-permute-start.2 = (bf16[4,512,256]{1,2,0:T(8,128)(2,1)S(1)}, bf16[4,512,256]{1,2,0:T(8,128)(2,1)}, u32[]{:S(2)}, u32[]{:S(2)}) collective-permute-start(bf16[4,512,256]{1,2,0:T(8,128)(2,1)S(1)} %pad_maximum_fusion.1), channel_id=1, source_target_pairs={{0,4},{1,5},{2,6},{3,7},{4,0},{5,1},{6,2},{7,3},{8,12},{9,13},{10,... | collective-permute-start | bytes 3145736 | tf_op jit(solution)/shard_map/ppermute | solution.py:11
  147.9 1.0 copy-start.1
  147.9 1.1 copy-start.4
  245.7 2.4 copy-start.5
Sparse Core Ops, SparseCore 0:
  151.2 81.3 all-reduce.1
where the time goes:
time: 260 us; the launch traced here: 255 us
  blocking collectives  182 us (70%)
  waiting for transfers between devices  35.9 us (14%)
  between operations  14.2 us (5%)
  other arithmetic  7.69 us (3%)
  matrix products  6.62 us (3%)
  starting transfers between devices  4.69 us (2%)
  local copies, waits for them, and re-layouts  4.18 us (2%)
    all_to_all x1, blocking collectives, local(): lax.all_to_all(outgoing, 'expert', split_axis=0, concat_axis=0, tiled=True)  90.3 us
    psum x1, blocking collectives, local(): totals = lax.psum(local_counts, ('dp', 'expert'))  79.7 us
    ppermute x3, waiting for transfers between devices, swapped(): lax.ppermute(array, axis, [(i, i ^ 1 << stride) for i in range(lax.axis_s...  35.9 us
    psum x1, blocking collectives, local(): merged, summed = lax.psum((gram_block, column_sums), 'dp')  11.7 us
  transfers between devices with their start and end apart: 4, of which 3 were waited for; matrix products, arithmetic and copies ran while one was open for 1% of the time, Pallas kernels for 0%

commit v1 on v0

v1 whole, which is shorter than its diff:
```python
import functools

import jax
import jax.numpy as jnp
from jax import lax
from jax.experimental import pallas as pl
from jax.experimental.pallas import tpu as pltpu
from jax.sharding import PartitionSpec as P

MESH = pl.DeviceIdType.MESH
F32 = jnp.float32
BF16 = jnp.bfloat16

CAP = 16
XS = 4
YS = 4
ZS = 8
FLAG = 128
CH = 2 * YS * CAP
COUNT_ROWS = 16


def kernel(
    tok_ref, routes_ref, slots_ref, wg_hbm, wu_hbm, cov_ref, mean_ref,
    packed, rows, wg, wu, hid, hidz, gram, colsum,
    w_sem, l_sem, x_s, x_r, ya_s, ya_r, yb_s, yb_r, sb_s, sb_r,
    z_s, z_r, h_s, h_r, hs_s,
):
    depth = wg.shape[0]
    units = wg.shape[1]
    wide = depth + FLAG
    half = depth // 2
    chunks = XS

    z = lax.axis_index("dp")
    member = lax.axis_index("expert")
    x = member // (2 * YS)
    y = (member // 2) % YS
    c = member % 2

    def dev(dx=0, dy=0, dz=0, dc=0):
        xx = (x + dx) % XS
        yy = (y + dy) % YS
        cc = (c + dc) % 2
        return {"dp": (z + dz) % ZS, "expert": (xx * YS + yy) * 2 + cc}

    peers = [dict(dx=1), dict(dx=2), dict(dx=3), dict(dy=1), dict(dy=3), dict(dc=1), dict(dz=1), dict(dz=7)]
    barrier = pltpu.get_barrier_semaphore()
    for p in peers:
        pl.semaphore_signal(barrier, inc=1, device_id=dev(**p), device_id_type=MESH)
    wg_copy = pltpu.make_async_copy(wg_hbm, wg, w_sem.at[0])
    wu_copy = pltpu.make_async_copy(wu_hbm, wu, w_sem.at[1])
    wg_copy.start()
    wu_copy.start()

    routes = routes_ref[...]
    slots = slots_ref[...]
    usable = (routes < XS) & (slots < CAP)
    target = jnp.where(usable, routes * CAP + slots, -1)
    tok_rows = routes.shape[0]
    places = lax.broadcasted_iota(jnp.int32, (tok_rows, XS * CAP), 1)
    hit = jnp.zeros((tok_rows, XS * CAP), F32)
    for k in range(routes.shape[1]):
        hit = jnp.maximum(hit, jnp.where(target[:, k : k + 1] == places, 1.0, 0.0))
    placing = hit.astype(BF16)

    def tdot(a, b):
        return lax.dot_general(a, b, (((0,), (0,)), ((), ())), preferred_element_type=F32)

    step = depth // 7
    for j in range(7):
        part = tdot(placing, tok_ref[:, j * step : (j + 1) * step]).astype(BF16)
        for g in range(XS):
            packed[g, :, j * step : (j + 1) * step] = part[g * CAP : (g + 1) * CAP]
    flags = tdot(placing, jnp.ones((tok_rows, FLAG), BF16)).astype(BF16)
    for g in range(XS):
        packed[g, :, depth:wide] = flags[g * CAP : (g + 1) * CAP]

    pl.semaphore_wait(barrier, len(peers))

    sends = []

    def send(src, dst, ss, rs, to):
        copy = pltpu.make_async_remote_copy(
            src_ref=src, dst_ref=dst, send_sem=ss, recv_sem=rs, device_id=to, device_id_type=MESH
        )
        copy.start()
        return copy

    def arrived(dst, rs):
        pltpu.make_async_remote_copy(
            src_ref=dst, dst_ref=dst, send_sem=rs, recv_sem=rs, device_id=dev(dc=1), device_id_type=MESH
        ).wait_recv()

    def piece(k, yy, cc):
        start = pl.multiple_of((yy * 2 + cc) * CAP, CAP)
        return rows.at[k, pl.ds(start, CAP), :]

    def half_piece(k, yy, cc, h):
        start = pl.multiple_of((yy * 2 + cc) * CAP, CAP)
        lanes = pl.ds(0, half) if h == 0 else pl.ds(half, wide - half)
        return rows.at[k, pl.ds(start, CAP), lanes]

    y_up, y_dn, y_op = (y + 1) % YS, (y + YS - 1) % YS, (y + 2) % YS

    def stage_a(k):
        if k == 0:
            own = packed.at[x]
        else:
            own = piece(k, y, c)
            arrived(own, x_r.at[k - 1])
        sends.append(send(own, piece(k, y, c), ya_s.at[k, 0], ya_r.at[k, 0], dev(dy=1)))
        sends.append(send(own, piece(k, y, c), ya_s.at[k, 1], ya_r.at[k, 1], dev(dy=3)))
        sends.append(send(own, piece(k, y, c), sb_s.at[k, 0], sb_r.at[k, 0], dev(dc=1)))

    def stage_b(k):
        arrived(piece(k, y_dn, c), ya_r.at[k, 0])
        sends.append(send(half_piece(k, y_dn, c, 0), half_piece(k, y_dn, c, 0), yb_s.at[k, 0], yb_r.at[k, 0], dev(dy=1)))
        sends.append(send(piece(k, y_dn, c), piece(k, y_dn, c), sb_s.at[k, 1], sb_r.at[k, 1], dev(dc=1)))
        arrived(piece(k, y_up, c), ya_r.at[k, 1])
        sends.append(send(half_piece(k, y_up, c, 1), half_piece(k, y_up, c, 1), yb_s.at[k, 1], yb_r.at[k, 1], dev(dy=3)))
        sends.append(send(piece(k, y_up, c), piece(k, y_up, c), sb_s.at[k, 2], sb_r.at[k, 2], dev(dc=1)))

    def stage_c(k):
        arrived(half_piece(k, y_op, c, 0), yb_r.at[k, 0])
        arrived(half_piece(k, y_op, c, 1), yb_r.at[k, 1])
        sends.append(send(piece(k, y_op, c), piece(k, y_op, c), sb_s.at[k, 3], sb_r.at[k, 3], dev(dc=1)))

    def hrows(k):
        n = CH + (COUNT_ROWS if k == chunks - 1 else 0)
        return pl.ds(k * CH, n)

    def hslot(k, s):
        return hid.at[s, hrows(k), :]

    def hhalf(k, h):
        n = CH // 2 + (COUNT_ROWS if (k == chunks - 1 and h == 1) else 0)
        return hid.at[4, pl.ds(k * CH + h * (CH // 2), n), :]

    def hhalf_of(k, s, h):
        n = CH // 2 + (COUNT_ROWS if (k == chunks - 1 and h == 1) else 0)
        return hid.at[s, pl.ds(k * CH + h * (CH // 2), n), :]

    def stage_d(k):
        for i, yy in enumerate((y, y_dn, y_up, y_op)):
            arrived(piece(k, yy, (c + 1) % 2), sb_r.at[k, i])
        if k == 0:
            wg_copy.wait()
            wu_copy.wait()
        lhs = rows[k, :, 0:depth]
        gate = jnp.dot(lhs, wg[...], preferred_element_type=F32)
        up = jnp.dot(lhs, wu[...], preferred_element_type=F32)
        hid[0, k * CH : (k + 1) * CH, :] = (gate / (1.0 + jnp.exp(-gate)) * up).astype(BF16)
        if k == chunks - 1:
            for r in range(chunks):
                used = jnp.sum(rows[r, :, depth:wide].astype(F32), axis=0, keepdims=True)
                used = jnp.concatenate([used, used], axis=1)
                hid[0, chunks * CH + 4 * r : chunks * CH + 4 * (r + 1), :] = jnp.broadcast_to(used, (4, units)).astype(BF16)
        sends.append(send(hslot(k, 0), hslot(k, 1), z_s.at[k, 0, 0], z_r.at[k, 0, 0], dev(dz=1)))
        sends.append(send(hslot(k, 0), hslot(k, 7), z_s.at[k, 0, 1], z_r.at[k, 0, 1], dev(dz=7)))

    def stage_z(k, t):
        arrived(hslot(k, t), z_r.at[k, t - 1, 0])
        if t < 3:
            sends.append(send(hslot(k, t), hslot(k, t + 1), z_s.at[k, t, 0], z_r.at[k, t, 0], dev(dz=1)))
        else:
            sends.append(send(hhalf_of(k, 3, 0), hhalf(k, 0), z_s.at[k, 3, 0], z_r.at[k, 3, 0], dev(dz=1)))
        arrived(hslot(k, 8 - t), z_r.at[k, t - 1, 1])
        if t < 3:
            sends.append(send(hslot(k, 8 - t), hslot(k, 7 - t), z_s.at[k, t, 1], z_r.at[k, t, 1], dev(dz=7)))
        else:
            sends.append(send(hhalf_of(k, 5, 1), hhalf(k, 1), z_s.at[k, 3, 1], z_r.at[k, 3, 1], dev(dz=7)))

    def stage_z5(k):
        arrived(hhalf(k, 0), z_r.at[k, 3, 0])
        arrived(hhalf(k, 1), z_r.at[k, 3, 1])

    d = (y + YS - z // 2) % YS
    on_line = c == z % 2

    def bpart(ref, k, h):
        return ref.at[pl.ds(4 * h, 4), pl.ds(k * CH, CH), :]

    def bcopy(src, k, h, to_y):
        if to_y:
            ss, to = h_s.at[k, h], dev(dy=1 if h == 0 else 3)
        else:
            ss, to = hs_s.at[k, h], dev(dc=1)
        return pltpu.make_async_remote_copy(
            src_ref=bpart(src, k, h), dst_ref=bpart(hidz, k, h), send_sem=ss, recv_sem=h_r.at[k, h],
            device_id=to, device_id_type=MESH,
        )

    def own_copy(k):
        return pltpu.make_async_copy(
            hid.at[:, pl.ds(k * CH, CH), :], hidz.at[:, pl.ds(k * CH, CH), :], l_sem.at[k]
        )

    def bforward(k, h, to_y):
        arrived(bpart(hidz, k, h), h_r.at[k, h])
        if to_y:
            bcopy(hidz, k, h, True).start()
        bcopy(hidz, k, h, False).start()

    def stage_y1(k):
        @pl.when(on_line & (d == 0))
        def _():
            for h in range(2):
                bcopy(hid, k, h, True).start()
            for h in range(2):
                bcopy(hid, k, h, False).start()
            own_copy(k).start()

    def stage_y2(k):
        @pl.when(on_line & (d == 1))
        def _():
            bforward(k, 0, True)

        @pl.when(on_line & (d == 3))
        def _():
            bforward(k, 1, True)

    def stage_y3(k):
        @pl.when(on_line & (d == 2))
        def _():
            bforward(k, 0, True)
            bforward(k, 1, True)

    def stage_y4(k):
        @pl.when(on_line & (d == 1))
        def _():
            bforward(k, 1, False)

        @pl.when(on_line & (d == 3))
        def _():
            bforward(k, 0, False)

        @pl.when(on_line & (d == 0))
        def _():
            own_copy(k).wait()

        @pl.when(jnp.logical_not(on_line))
        def _():
            arrived(bpart(hidz, k, 0), h_r.at[k, 0])
            arrived(bpart(hidz, k, 1), h_r.at[k, 1])

        n = ZS * CH
        a = hid[:, k * CH : (k + 1) * CH, :].reshape(n, units)
        b = hidz[:, k * CH : (k + 1) * CH, :].reshape(n, units)
        ones_l = jnp.ones((n, 128), BF16)
        ones_s = jnp.ones((8, n), BF16)
        g_part = tdot(a, jnp.concatenate([b, ones_l], axis=1))
        s_part = jnp.dot(ones_s, jnp.concatenate([a, b], axis=1), preferred_element_type=F32)
        if k == 0:
            gram[...] = g_part
            colsum[...] = s_part
        else:
            gram[...] += g_part
            colsum[...] += s_part

    stage_a(0)
    for k, dx in ((1, 1), (2, 3), (3, 2)):
        sends.append(send(packed.at[(x + dx) % XS], piece(k, y, c), x_s.at[k - 1], x_r.at[k - 1], dev(dx=dx)))
    own_rows = pl.multiple_of((y * 2 + c) * CAP, CAP)
    rows[0, pl.ds(own_rows, CAP), :] = packed[x]

    stage_a(1)
    stage_b(0)
    stage_a(2)
    stage_c(0)
    stage_d(0)

    stage_b(1)
    stage_a(3)
    stage_z(0, 1)
    stage_c(1)
    stage_z(0, 2)
    stage_d(1)
    stage_z(0, 3)

    stage_b(2)
    stage_z5(0)
    stage_y1(0)
    stage_z(1, 1)
    stage_c(2)
    stage_y2(0)
    stage_z(1, 2)
    stage_d(2)
    stage_y3(0)
    stage_z(1, 3)

    stage_b(3)
    stage_z5(1)
    stage_y1(1)
    stage_z(2, 1)
    stage_c(3)
    stage_y2(1)
    stage_z(2, 2)
    stage_d(3)
    stage_y4(0)
    stage_y3(1)
    stage_z(2, 3)

    stage_z5(2)
    stage_y1(2)
    stage_z(3, 1)
    stage_y2(2)
    stage_y4(1)
    stage_z(3, 2)
    stage_y3(2)
    stage_z(3, 3)
    stage_y4(2)
    stage_z5(3)
    stage_y1(3)
    stage_y2(3)
    stage_y3(3)
    stage_y4(3)

    used = hid[:, chunks * CH : chunks * CH + COUNT_ROWS, 0:128].astype(F32)
    count = jnp.sum(used) * (1.0 / (4 * 128))
    mean_ref[...] = colsum[:, 0:units] / count
    row_mean = gram[:, units : units + 1] / count
    col_mean = colsum[0:1, units:] / count
    cov_ref[...] = gram[:, 0:units] / count - row_mean * col_mean

    for copy in sends:
        copy.wait_send()
    for k in range(chunks):
        @pl.when(on_line & (d != 3))
        def _():
            bcopy(hidz, k, 0, True).wait_send()

        @pl.when(on_line & (d != 1))
        def _():
            bcopy(hidz, k, 1, True).wait_send()

        @pl.when(on_line)
        def _():
            bcopy(hidz, k, 0, False).wait_send()
            bcopy(hidz, k, 1, False).wait_send()


def local(tokens, routes, slots, gate_weight, up_weight):
    tok_rows, depth = tokens.shape
    units = gate_weight.shape[1]
    hrows = XS * CH + COUNT_ROWS
    vmem = pl.BlockSpec(memory_space=pltpu.VMEM)
    hbm = pl.BlockSpec(memory_space=pl.ANY)
    dma = pltpu.SemaphoreType.DMA
    cov, means = pl.pallas_call(
        kernel,
        out_shape=(
            jax.ShapeDtypeStruct((units, units), F32),
            jax.ShapeDtypeStruct((8, units), F32),
        ),
        in_specs=[vmem, vmem, vmem, hbm, hbm],
        out_specs=(vmem, vmem),
        scratch_shapes=[
            pltpu.VMEM((XS, CAP, depth + FLAG), BF16),
            pltpu.VMEM((XS, CH, depth + FLAG), BF16),
            pltpu.VMEM((depth, units), BF16),
            pltpu.VMEM((depth, units), BF16),
            pltpu.VMEM((ZS, hrows, units), BF16),
            pltpu.VMEM((ZS, hrows, units), BF16),
            pltpu.VMEM((units, units + 128), F32),
            pltpu.VMEM((8, 2 * units), F32),
            dma((2,)), dma((XS,)),
            dma((3,)), dma((3,)),
            dma((XS, 2)), dma((XS, 2)),
            dma((XS, 2)), dma((XS, 2)),
            dma((XS, 4)), dma((XS, 4)),
            dma((XS, 4, 2)), dma((XS, 4, 2)),
            dma((XS, 2)), dma((XS, 2)), dma((XS, 2)),
        ],
        compiler_params=pltpu.CompilerParams(
            collective_id=0, has_side_effects=True, vmem_limit_bytes=48 << 20
        ),
        name="moments",
    )(tokens, routes, slots, gate_weight, up_weight)
    return means[0], cov


def solution(mesh):
    in_specs = (
        P(("dp", "expert"), None),
        P(("dp", "expert"), None),
        P(("dp", "expert"), None),
        P(None, "expert"),
        P(None, "expert"),
    )
    out_specs = (P("expert"), P("expert", "dp"))
    return jax.shard_map(local, mesh=mesh, in_specs=in_specs, out_specs=out_specs, check_vma=False)
```

time: 260 us -> 109 us (0.42); the launches traced: 255 us -> 109 us
  blocking collectives: 182 us -> 0 us
  Pallas kernels: 0 us -> 102 us
  waiting for transfers between devices: 35.9 us -> 0 us
  between operations: 14.2 us -> 0.65 us
  other arithmetic: 7.69 us -> 0 us
  matrix products: 6.62 us -> 0 us
  starting transfers between devices: 4.69 us -> 0 us
    pallas_call x0 -> x1, Pallas kernels: none -> 102 us  [local(): pl.pallas_call(kernel, out_shape=(jax.ShapeDtypeStruct((units, units), F3...]
    psum x2 -> x0, blocking collectives: 91.4 us -> none  [the longest x1 79.7 us: local(): totals = lax.psum(local_counts, ('dp', 'expert'))]
    all_to_all x1 -> x0, blocking collectives: 90.3 us -> none  [local(): lax.all_to_all(outgoing, 'expert', split_axis=0, concat_axis=0, tiled=True)]
    ppermute x3 -> x0, waiting for transfers between devices: 35.9 us -> none  [swapped(): lax.ppermute(array, axis, [(i, i ^ 1 << stride) for i in range(lax.axis_s...]
    dot_general x4 -> x0, matrix products: 6.62 us -> none  [the longest x1 2.12 us: local(): jnp.einsum('scd,du->scu', arrived, up_weight, preferred_element_type=jnp....]
    ppermute x3 -> x0, starting transfers between devices: 4.65 us -> none  [swapped(): lax.ppermute(array, axis, [(i, i ^ 1 << stride) for i in range(lax.axis_s...]
    unnamed x17 -> x7, local copies, waits for them, and re-layouts: 2.34 us -> 5.81 us
  transfers between devices with their start and end apart: 4 -> 0, of which waited for: 3 -> 0; matrix products, arithmetic and copies ran while one was open for 1% -> 0% of each run, Pallas kernels for 0% -> 0%
where the time goes in v1:
time: 109 us
  Pallas kernels  102 us (94%)
  local copies, waits for them, and re-layouts  6.37 us (6%)
    pallas_call x1, Pallas kernels, local(): pl.pallas_call(kernel, out_shape=(jax.ShapeDtypeStruct((units, units), F3...  102 us
    unnamed x7, local copies, waits for them, and re-layouts  5.81 us

profile of v1, /device:TPU:9, one launch (start us, length us, event | category | flops | bytes accessed | tf_op | source)
XLA Modules:
  0.0 108.9 jit_solution(17456062108015882095)
XLA Ops:
  0.6 0.8 copy.7.routes_ref
  1.4 0.8 copy.8.slots_ref
  2.2 0.0 copy-start
  2.2 2.0 %copy-done = bf16[7168,256]{1,0:T(8,128)(2,1)S(1)} copy-done((bf16[7168,256]{1,0:T(8,128)(2,1)S(1)}, bf16[7168,256]{1,0:T(8,128)(2,1)}, u32[]{:S(2)}) %copy-start) | copy-done | bytes 3670040
  4.2 0.0 copy-start.1
  4.2 1.5 %copy-done.1 = bf16[128,7168]{1,0:T(8,128)(2,1)S(1)} copy-done((bf16[128,7168]{1,0:T(8,128)(2,1)S(1)}, bf16[128,7168]{1,0:T(8,128)(2,1)}, u32[]{:S(2)}) %copy-start.1) | copy-done | bytes 1835032
  5.7 101.8 %moments.1 = (f32[256,256]{1,0:T(8,128)S(1)}, f32[8,256]{1,0:T(8,128)S(1)}) custom-call(bf16[128,7168]{1,0:T(8,128)(2,1)S(1)} %copy-done.1, s32[128,8]{1,0:T(8,128)S(1)} %copy.7.routes_ref, s32[128,8]{1,0:T(8,128)S(1)} %copy.8.slots_ref, bf16[7168,256]{1,0:T(8,128)(2,1)S(1)} %copy-done, bf16[7168,256]{1,0:T(8,128)(2,1)} %wu_hbm.1), custom_call_target="tpu_custom_call" | custom-call | tf_op jit(solution)/shard_map/moments/pallas_call | solution.py:350
  107.6 0.6 slice.3
  108.2 0.7 copy.10
Async XLA Ops:
  2.2 2.0 %copy-start = (bf16[7168,256]{1,0:T(8,128)(2,1)S(1)}, bf16[7168,256]{1,0:T(8,128)(2,1)}, u32[]{:S(2)}) copy-start(bf16[7168,256]{1,0:T(8,128)(2,1)} %wg_hbm.1) | copy-start | bytes 11010052
  4.2 1.5 %copy-start.1 = (bf16[128,7168]{1,0:T(8,128)(2,1)S(1)}, bf16[128,7168]{1,0:T(8,128)(2,1)}, u32[]{:S(2)}) copy-start(bf16[128,7168]{1,0:T(8,128)(2,1)} %tok_ref.1) | copy-start | bytes 5505028

commit v2 on v1

v2 whole, which is shorter than its diff:
```python
import functools

import jax
import jax.numpy as jnp
from jax import lax
from jax.experimental import pallas as pl
from jax.experimental.pallas import tpu as pltpu
from jax.sharding import PartitionSpec as P

MESH = pl.DeviceIdType.MESH
F32 = jnp.float32
BF16 = jnp.bfloat16

CAP = 16
XS = 4
YS = 4
ZS = 8
FLAG = 128
CHUNKS = ((0, 0, 16, 0), (1, 0, 16, 128), (3, 0, 16, 256), (2, 0, 8, 384), (2, 8, 8, 448))
ROWS = 2 * XS * YS * CAP
COUNT_ROWS = 16


RELAY = (0, 1)
DIRECT = tuple(k for k in range(len(CHUNKS)) if k not in RELAY)
STRAIGHT = (4,)


def kernel(
    tok_ref, routes_ref, slots_ref, wg_hbm, wu_hbm, cov_ref, mean_ref,
    packed, rows, wg, wu, hid, hidz, hidy, gram, colsum,
    w_sem, l_sem, x_s, x_r, ya_s, ya_r, yb_s, yb_r, sb_s, sb_r,
    z_s, z_r, zd_s, zd_r, h_s, h_r, hs_s, ye_s, ye_r, e_s, e_r, t_s, t_r,
):
    depth = wg.shape[0]
    units = wg.shape[1]
    wide = depth + FLAG
    half = depth // 2
    last = len(CHUNKS) - 1

    z = lax.axis_index("dp")
    member = lax.axis_index("expert")
    x = member // (2 * YS)
    y = (member // 2) % YS
    c = member % 2

    def dev(dx=0, dy=0, dz=0, dc=0):
        xx = (x + dx) % XS
        yy = (y + dy) % YS
        cc = (c + dc) % 2
        return {"dp": (z + dz) % ZS, "expert": (xx * YS + yy) * 2 + cc}

    peers = [dict(dx=1), dict(dx=2), dict(dx=3), dict(dy=1), dict(dy=2), dict(dy=3), dict(dc=1)]
    peers += [dict(dz=s) for s in range(1, ZS)]
    barrier = pltpu.get_barrier_semaphore()
    for p in peers:
        pl.semaphore_signal(barrier, inc=1, device_id=dev(**p), device_id_type=MESH)
    on_line = c == z % 2
    wg_copy = pltpu.make_async_copy(wg_hbm, wg, w_sem.at[0])
    wu_copy = pltpu.make_async_copy(wu_hbm, wu, w_sem.at[1])
    wg_copy.start()
    wu_copy.start()

    routes = routes_ref[...]
    slots = slots_ref[...]
    usable = (routes < XS) & (slots < CAP)
    target = jnp.where(usable, routes * CAP + slots, -1)
    tok_rows = routes.shape[1]
    places = lax.broadcasted_iota(jnp.int32, (XS * CAP, tok_rows), 0)
    hit = jnp.zeros((XS * CAP, tok_rows), F32)
    for k in range(routes.shape[0]):
        hit = jnp.maximum(hit, jnp.where(target[k : k + 1, :] == places, 1.0, 0.0))
    placing = hit.astype(BF16)

    def tdot(a, b):
        return lax.dot_general(a, b, (((0,), (0,)), ((), ())), preferred_element_type=F32)

    step = depth // 7
    for j in range(7):
        part = jnp.dot(placing, tok_ref[:, j * step : (j + 1) * step], preferred_element_type=F32).astype(BF16)
        for g in range(XS):
            packed[g, :, j * step : (j + 1) * step] = part[g * CAP : (g + 1) * CAP]
    flags = jnp.dot(placing, jnp.ones((tok_rows, FLAG), BF16), preferred_element_type=F32).astype(BF16)
    for g in range(XS):
        packed[g, :, depth:wide] = flags[g * CAP : (g + 1) * CAP]

    gram[...] = jnp.zeros_like(gram)
    colsum[...] = jnp.zeros_like(colsum)
    pl.semaphore_wait(barrier, len(peers))

    sends = []

    def send(src, dst, ss, rs, to):
        copy = pltpu.make_async_remote_copy(
            src_ref=src, dst_ref=dst, send_sem=ss, recv_sem=rs, device_id=to, device_id_type=MESH
        )
        copy.start()
        return copy

    def arrived(dst, rs):
        pltpu.make_async_remote_copy(
            src_ref=dst, dst_ref=dst, send_sem=rs, recv_sem=rs, device_id=dev(dc=1), device_id_type=MESH
        ).wait_recv()

    def size(k):
        return 2 * YS * CHUNKS[k][2]

    def piece_rows(k, yy, cc):
        n = CHUNKS[k][2]
        return pl.ds(pl.multiple_of(CHUNKS[k][3] + (yy * 2 + cc) * n, n), n)

    def lanes(h):
        return pl.ds(0, half) if h == 0 else pl.ds(half, wide - half)

    def piece(k, yy, cc):
        return rows.at[piece_rows(k, yy, cc), :]

    def half_piece(k, yy, cc, h):
        return rows.at[piece_rows(k, yy, cc), lanes(h)]

    y_up, y_dn, y_op = (y + 1) % YS, (y + YS - 1) % YS, (y + 2) % YS

    def stage_a(k):
        dx, lo, n, _ = CHUNKS[k]
        if dx == 0:
            own = packed.at[x, pl.ds(lo, n), :]
        else:
            own = piece(k, y, c)
            arrived(own, x_r.at[k])
        for i in range(2):
            for way in range(2):
                h = way if i == 0 else 1 - way
                src = packed.at[x, pl.ds(lo, n), lanes(h)] if dx == 0 else half_piece(k, y, c, h)
                to = dev(dy=1 if way == 0 else 3)
                sends.append(send(src, half_piece(k, y, c, h), ya_s.at[k, way, i], ya_r.at[k, way, i], to))
        sends.append(send(own, piece(k, y, c), sb_s.at[k, 0], sb_r.at[k, 0], dev(dc=1)))

    def stage_b(k):
        for way, yy in enumerate((y_dn, y_up)):
            part = half_piece(k, yy, c, way)
            arrived(part, ya_r.at[k, way, 0])
            sends.append(send(part, part, yb_s.at[k, way], yb_r.at[k, way], dev(dy=1 if way == 0 else 3)))

    def stage_s(k):
        for way, yy in enumerate((y_dn, y_up)):
            arrived(half_piece(k, yy, c, 1 - way), ya_r.at[k, way, 1])
            sends.append(send(piece(k, yy, c), piece(k, yy, c), sb_s.at[k, 1 + way], sb_r.at[k, 1 + way], dev(dc=1)))

    def stage_c(k):
        arrived(half_piece(k, y_op, c, 0), yb_r.at[k, 0])
        arrived(half_piece(k, y_op, c, 1), yb_r.at[k, 1])
        sends.append(send(piece(k, y_op, c), piece(k, y_op, c), sb_s.at[k, 3], sb_r.at[k, 3], dev(dc=1)))

    def hrows(k):
        return pl.ds(CHUNKS[k][3], size(k) + (COUNT_ROWS if k == last else 0))

    def hslot(k, s):
        return hid.at[s, hrows(k), :]

    def hhalf(k, s, h):
        n = size(k) // 2
        return hid.at[s, pl.ds(CHUNKS[k][3] + h * n, n + (COUNT_ROWS if k == last and h == 1 else 0)), :]

    def stage_d(k):
        for i, yy in enumerate((y, y_dn, y_up, y_op)):
            arrived(piece(k, yy, (c + 1) % 2), sb_r.at[k, i])
        if k == 0:
            wg_copy.wait()
            wu_copy.wait()
        at, n = CHUNKS[k][3], size(k)
        lhs = rows[at : at + n, 0:depth]
        gate = jnp.dot(lhs, wg[...], preferred_element_type=F32)
        up = jnp.dot(lhs, wu[...], preferred_element_type=F32)
        hid[0, at : at + n, :] = (gate / (1.0 + jnp.exp(-gate)) * up).astype(BF16)
        if k == last:
            for r in range(4):
                part = ROWS // 4
                used = jnp.sum(rows[r * part : (r + 1) * part, depth:wide].astype(F32), axis=0, keepdims=True)
                used = jnp.concatenate([used, used], axis=1)
                hid[0, ROWS + 4 * r : ROWS + 4 * (r + 1), :] = jnp.broadcast_to(used, (4, units)).astype(BF16)
        if k in STRAIGHT:
            for s in (4, 3, 5, 2, 6, 1, 7):
                sends.append(send(hslot(k, 0), hslot(k, s), zd_s.at[k, s - 1], zd_r.at[k, s - 1], dev(dz=s)))
        else:
            sends.append(send(hslot(k, 0), hslot(k, 1), z_s.at[k, 0, 0], z_r.at[k, 0, 0], dev(dz=1)))
            sends.append(send(hslot(k, 0), hslot(k, 7), z_s.at[k, 0, 1], z_r.at[k, 0, 1], dev(dz=7)))

    def stage_q(k):
        for s in range(1, ZS):
            arrived(hslot(k, s), zd_r.at[k, s - 1])

    def stage_z(k, t):
        arrived(hslot(k, t), z_r.at[k, t - 1, 0])
        if t < 3:
            sends.append(send(hslot(k, t), hslot(k, t + 1), z_s.at[k, t, 0], z_r.at[k, t, 0], dev(dz=1)))
        else:
            sends.append(send(hhalf(k, 3, 0), hhalf(k, 4, 0), z_s.at[k, 3, 0], z_r.at[k, 3, 0], dev(dz=1)))
        arrived(hslot(k, 8 - t), z_r.at[k, t - 1, 1])
        if t < 3:
            sends.append(send(hslot(k, 8 - t), hslot(k, 7 - t), z_s.at[k, t, 1], z_r.at[k, t, 1], dev(dz=7)))
        else:
            sends.append(send(hhalf(k, 5, 1), hhalf(k, 4, 1), z_s.at[k, 3, 1], z_r.at[k, 3, 1], dev(dz=7)))

    def stage_z5(k):
        arrived(hhalf(k, 4, 0), z_r.at[k, 3, 0])
        arrived(hhalf(k, 4, 1), z_r.at[k, 3, 1])

    def accumulate(k):
        at, n = CHUNKS[k][3], ZS * size(k)
        a = hid[:, at : at + size(k), :].reshape(n, units)
        b = hidz[:, at : at + size(k), :].reshape(n, units)
        ones_l = jnp.ones((n, 128), BF16)
        ones_s = jnp.ones((8, n), BF16)
        gram[...] += tdot(a, jnp.concatenate([b, ones_l], axis=1))
        colsum[...] += jnp.dot(ones_s, jnp.concatenate([a, b], axis=1), preferred_element_type=F32)

    d = (y + YS - z // 2) % YS

    def bpart(ref, k, h):
        return ref.at[pl.ds(4 * h, 4), pl.ds(CHUNKS[k][3], size(k)), :]

    def bcopy(src, k, h, to_y):
        if to_y:
            ss, to = h_s.at[k, h], dev(dy=1 if h == 0 else 3)
        else:
            ss, to = hs_s.at[k, h], dev(dc=1)
        return pltpu.make_async_remote_copy(
            src_ref=bpart(src, k, h), dst_ref=bpart(hidz, k, h), send_sem=ss, recv_sem=h_r.at[k, h],
            device_id=to, device_id_type=MESH,
        )

    def own_copy(k):
        return pltpu.make_async_copy(
            hid.at[:, pl.ds(CHUNKS[k][3], size(k)), :], hidz.at[:, pl.ds(CHUNKS[k][3], size(k)), :], l_sem.at[k]
        )

    def bforward(k, h, to_y):
        arrived(bpart(hidz, k, h), h_r.at[k, h])
        if to_y:
            bcopy(hidz, k, h, True).start()
        bcopy(hidz, k, h, False).start()

    def stage_y1(k):
        @pl.when(on_line & (d == 0))
        def _():
            for h in range(2):
                bcopy(hid, k, h, True).start()
            for h in range(2):
                bcopy(hid, k, h, False).start()
            own_copy(k).start()

    def stage_y2(k):
        @pl.when(on_line & (d == 1))
        def _():
            bforward(k, 0, True)

        @pl.when(on_line & (d == 3))
        def _():
            bforward(k, 1, True)

    def stage_y3(k):
        @pl.when(on_line & (d == 2))
        def _():
            bforward(k, 0, True)
            bforward(k, 1, True)

    def stage_y4(k):
        @pl.when(on_line & (d == 1))
        def _():
            bforward(k, 1, False)

        @pl.when(on_line & (d == 3))
        def _():
            bforward(k, 0, False)

        @pl.when(on_line & (d == 0))
        def _():
            own_copy(k).wait()

        @pl.when(jnp.logical_not(on_line))
        def _():
            arrived(bpart(hidz, k, 0), h_r.at[k, 0])
            arrived(bpart(hidz, k, 1), h_r.at[k, 1])

        accumulate(k)

    def krows(ref, k, s):
        return ref.at[s, pl.ds(CHUNKS[k][3], size(k)), :]

    def block_of(j):
        return 2 * ((y + j) % YS) + c

    def held(k, j):
        return krows(hid, k, 0) if j == 0 else krows(hidy, k, j - 1)

    def side_copy(k, i):
        return pltpu.make_async_remote_copy(
            src_ref=krows(hid, k, 0), dst_ref=krows(hidy, k, YS - i - 1), send_sem=ye_s.at[k, i - 1],
            recv_sem=ye_r.at[k, YS - i - 1], device_id=dev(dy=i), device_id_type=MESH,
        )

    def block_copy(k, j):
        block = block_of(j)
        slot = (block + ZS - z) % ZS
        return pltpu.make_async_remote_copy(
            src_ref=held(k, j), dst_ref=krows(hidz, k, slot), send_sem=e_s.at[k, j],
            recv_sem=e_r.at[k, slot], device_id={"dp": block, "expert": member}, device_id_type=MESH,
        )

    def kept_copy(k, j):
        return pltpu.make_async_copy(held(k, j), krows(hidz, k, 0), l_sem.at[k])

    def line_copy(k):
        part = hidz.at[:, pl.ds(CHUNKS[k][3], size(k)), :]
        return pltpu.make_async_remote_copy(
            src_ref=part, dst_ref=part, send_sem=t_s.at[k], recv_sem=t_r.at[k],
            device_id=dev(dc=1), device_id_type=MESH,
        )

    def pass_on(k, j):
        if j > 0:
            arrived(held(k, j), ye_r.at[k, j - 1])

        @pl.when(z == block_of(j))
        def _():
            kept_copy(k, j).start()

        @pl.when(z != block_of(j))
        def _():
            block_copy(k, j).start()

    def stage_e(k):
        for i in (1, 3, 2):
            side_copy(k, i).start()
        pass_on(k, 0)

    def stage_f(k):
        for j in (1, 3, 2):
            pass_on(k, j)

    def stage_w(k):
        @pl.when(on_line)
        def _():
            for s in range(1, ZS):
                arrived(krows(hidz, k, s), e_r.at[k, s])
            kept_copy(k, 0).wait()
            line_copy(k).start()

    def stage_g(k):
        @pl.when(jnp.logical_not(on_line))
        def _():
            line_copy(k).wait_recv()

        accumulate(k)

    stage_a(0)
    for k, (dx, lo, n, _) in enumerate(CHUNKS):
        if dx > 0:
            src = packed.at[(x + dx) % XS, pl.ds(lo, n), :]
            sends.append(send(src, piece(k, y, c), x_s.at[k], x_r.at[k], dev(dx=dx)))
        else:
            rows[piece_rows(k, y, c), :] = packed[x, lo : lo + n]

    stage_b(0)
    stage_s(0)
    stage_a(1)
    stage_c(0)
    stage_b(1)
    stage_d(0)
    stage_a(2)
    stage_s(1)
    stage_a(3)
    stage_c(1)
    stage_z(0, 1)
    stage_d(1)
    stage_b(2)
    stage_a(4)
    stage_z(0, 2)
    stage_z(1, 1)
    stage_b(3)
    stage_s(2)
    stage_z(0, 3)
    stage_c(2)
    stage_s(3)
    stage_z(1, 2)
    stage_b(4)
    stage_z5(0)
    stage_y1(0)
    stage_d(2)
    stage_c(3)
    stage_z(1, 3)
    stage_e(2)
    stage_s(4)
    stage_c(4)
    stage_d(3)
    stage_e(3)
    stage_z(2, 1)
    stage_d(4)
    stage_z(3, 1)
    stage_z5(1)
    stage_y1(1)
    stage_f(3)
    stage_y2(0)
    stage_e(4)
    stage_y2(1)
    stage_q(4)
    stage_f(2)
    stage_y3(0)
    stage_y3(1)
    stage_w(3)
    stage_z(2, 2)
    stage_z(3, 2)
    stage_f(4)
    stage_y4(0)
    stage_w(2)
    stage_z(2, 3)
    stage_z(3, 3)
    stage_y4(1)
    stage_w(4)
    stage_z5(2)
    stage_g(2)
    stage_z5(3)
    stage_g(3)
    stage_g(4)

    used = hid[:, ROWS : ROWS + COUNT_ROWS, 0:128].astype(F32)
    count = jnp.sum(used) * (1.0 / (4 * 128))
    mean_ref[...] = colsum[:, 0:units] / count
    row_mean = gram[:, units : units + 1] / count
    col_mean = colsum[0:1, units:] / count
    cov_ref[...] = gram[:, 0:units] / count - row_mean * col_mean

    for copy in sends:
        copy.wait_send()
    for k in RELAY:
        @pl.when(on_line & (d != 3))
        def _():
            bcopy(hidz, k, 0, True).wait_send()

        @pl.when(on_line & (d != 1))
        def _():
            bcopy(hidz, k, 1, True).wait_send()

        @pl.when(on_line)
        def _():
            bcopy(hidz, k, 0, False).wait_send()
            bcopy(hidz, k, 1, False).wait_send()
    for k in DIRECT:
        for i in (1, 2, 3):
            side_copy(k, i).wait_send()
        for j in range(YS):
            @pl.when(z != block_of(j))
            def _():
                block_copy(k, j).wait_send()

        @pl.when(on_line)
        def _():
            line_copy(k).wait_send()


def local(tokens, routes, slots, gate_weight, up_weight):
    tok_rows, depth = tokens.shape
    units = gate_weight.shape[1]
    hrows = ROWS + COUNT_ROWS
    nk = len(CHUNKS)
    vmem = pl.BlockSpec(memory_space=pltpu.VMEM)
    hbm = pl.BlockSpec(memory_space=pl.ANY)
    dma = pltpu.SemaphoreType.DMA
    cov, means = pl.pallas_call(
        kernel,
        out_shape=(
            jax.ShapeDtypeStruct((units, units), F32),
            jax.ShapeDtypeStruct((8, units), F32),
        ),
        in_specs=[vmem, vmem, vmem, hbm, hbm],
        out_specs=(vmem, vmem),
        scratch_shapes=[
            pltpu.VMEM((XS, CAP, depth + FLAG), BF16),
            pltpu.VMEM((ROWS, depth + FLAG), BF16),
            pltpu.VMEM((depth, units), BF16),
            pltpu.VMEM((depth, units), BF16),
            pltpu.VMEM((ZS, hrows, units), BF16),
            pltpu.VMEM((ZS, hrows, units), BF16),
            pltpu.VMEM((YS - 1, ROWS, units), BF16),
            pltpu.VMEM((units, units + 128), F32),
            pltpu.VMEM((8, 2 * units), F32),
            dma((2,)), dma((nk,)),
            dma((nk,)), dma((nk,)),
            dma((nk, 2, 2)), dma((nk, 2, 2)),
            dma((nk, 2)), dma((nk, 2)),
            dma((nk, 4)), dma((nk, 4)),
            dma((nk, 4, 2)), dma((nk, 4, 2)),
            dma((nk, ZS - 1)), dma((nk, ZS - 1)),
            dma((nk, 2)), dma((nk, 2)), dma((nk, 2)),
            dma((nk, YS - 1)), dma((nk, YS - 1)),
            dma((nk, YS)), dma((nk, ZS)),
            dma((nk,)), dma((nk,)),
        ],
        compiler_params=pltpu.CompilerParams(
            collective_id=0, has_side_effects=True, vmem_limit_bytes=60 << 20
        ),
        name="moments",
    )(tokens, routes.T, slots.T, gate_weight, up_weight)
    return means[0], cov


def solution(mesh):
    in_specs = (
        P(("dp", "expert"), None),
        P(("dp", "expert"), None),
        P(("dp", "expert"), None),
        P(None, "expert"),
        P(None, "expert"),
    )
    out_specs = (P("expert"), P("expert", "dp"))
    return jax.shard_map(local, mesh=mesh, in_specs=in_specs, out_specs=out_specs, check_vma=False)
```

time: 109 us -> 85.5 us (0.78)
  the two profiles are of different devices: /device:TPU:9 before, /device:TPU:17 now
where the time goes in v2:
time: 85.5 us; the launch traced here: 85.3 us
  Pallas kernels  81.7 us (96%)
  local copies, waits for them, and re-layouts  2.93 us (3%)
    pallas_call x1, Pallas kernels, local(): pl.pallas_call(kernel, out_shape=(jax.ShapeDtypeStruct((units, units), F3...  81.7 us

profile of v2, /device:TPU:17, one launch (start us, length us, event | category | flops | bytes accessed | tf_op | source)
XLA Modules:
  0.0 85.3 jit_solution(8662250755254218078)
XLA Ops:
  0.6 81.7 %moments.1 = (f32[256,256]{1,0:T(8,128)}, f32[8,256]{1,0:T(8,128)}) custom-call(bf16[128,7168]{1,0:T(8,128)(2,1)} %tok_ref.1, s32[8,128]{1,0:T(8,128)} %bitcast.3, s32[8,128]{1,0:T(8,128)} %bitcast.4, bf16[7168,256]{1,0:T(8,128)(2,1)} %wg_hbm.1, bf16[7168,256]{1,0:T(8,128)(2,1)} %wu_hbm.1), custom_call_target="tpu_custom_call" | custom-call | tf_op jit(solution)/shard_map/moments/pallas_call | solution.py:469
  82.4 1.3 %slice.3 = f32[1,256]{1,0:T(1,128)} slice(f32[8,256]{1,0:T(8,128)} %get-tuple-element.4), slice={[0:1], [0:256]} | slice | bytes 2048 | tf_op jit(solution)/shard_map/slice | solution.py:504
  83.6 1.7 %copy.8 = f32[256,256]{1,0:T(8,128)} copy(f32[256,256]{1,0:T(8,128)} %get-tuple-element.9) | data formatting | bytes 524288

commit v3 on v2

--- a/solution.py
+++ b/solution.py
@@ -16,19 +16,20 @@
 YS = 4
 ZS = 8
 FLAG = 128
-CHUNKS = ((0, 0, 16, 0), (1, 0, 16, 128), (3, 0, 16, 256), (2, 0, 8, 384), (2, 8, 8, 448))
+CHUNKS = ((0, 0, 16, 0), (1, 0, 16, 128), (3, 0, 16, 256), (2, 0, 16, 384))
 ROWS = 2 * XS * YS * CAP
 COUNT_ROWS = 16
 
 
 RELAY = (0, 1)
 DIRECT = tuple(k for k in range(len(CHUNKS)) if k not in RELAY)
-STRAIGHT = (4,)
+STRAIGHT = ()
+PAIRED = ()
 
 
 def kernel(
-    tok_ref, routes_ref, slots_ref, wg_hbm, wu_hbm, cov_ref, mean_ref,
-    packed, rows, wg, wu, hid, hidz, hidy, gram, colsum,
+    tok_hbm, routes_hbm, slots_hbm, wg_hbm, wu_hbm, cov_ref, mean_ref,
+    tok_ref, routes_ref, slots_ref, packed, rows, wg, wu, hid, hidz, hidy, gram, colsum,
     w_sem, l_sem, x_s, x_r, ya_s, ya_r, yb_s, yb_r, sb_s, sb_r,
     z_s, z_r, zd_s, zd_r, h_s, h_r, hs_s, ye_s, ye_r, e_s, e_r, t_s, t_r,
 ):
@@ -58,8 +59,18 @@
     on_line = c == z % 2
     wg_copy = pltpu.make_async_copy(wg_hbm, wg, w_sem.at[0])
     wu_copy = pltpu.make_async_copy(wu_hbm, wu, w_sem.at[1])
+    fetches = [
+        pltpu.make_async_copy(src, dst, w_sem.at[2 + i])
+        for i, (src, dst) in enumerate(((routes_hbm, routes_ref), (slots_hbm, slots_ref), (tok_hbm, tok_ref)))
+    ]
+    for copy in fetches:
+        copy.start()
     wg_copy.start()
     wu_copy.start()
+    gram[...] = jnp.zeros_like(gram)
+    colsum[...] = jnp.zeros_like(colsum)
+    for copy in fetches:
+        copy.wait()
 
     routes = routes_ref[...]
     slots = slots_ref[...]
@@ -84,8 +95,6 @@
     for g in range(XS):
         packed[g, :, depth:wide] = flags[g * CAP : (g + 1) * CAP]
 
-    gram[...] = jnp.zeros_like(gram)
-    colsum[...] = jnp.zeros_like(colsum)
     pl.semaphore_wait(barrier, len(peers))
 
     sends = []
@@ -181,6 +190,10 @@
         if k in STRAIGHT:
             for s in (4, 3, 5, 2, 6, 1, 7):
                 sends.append(send(hslot(k, 0), hslot(k, s), zd_s.at[k, s - 1], zd_r.at[k, s - 1], dev(dz=s)))
+        elif k in PAIRED:
+            for way, (near, far) in enumerate(((1, 2), (7, 6))):
+                sends.append(send(hslot(k, 0), hslot(k, far), z_s.at[k, 1, way], z_r.at[k, 1, way], dev(dz=far)))
+                sends.append(send(hslot(k, 0), hslot(k, near), z_s.at[k, 0, way], z_r.at[k, 0, way], dev(dz=near)))
         else:
             sends.append(send(hslot(k, 0), hslot(k, 1), z_s.at[k, 0, 0], z_r.at[k, 0, 0], dev(dz=1)))
             sends.append(send(hslot(k, 0), hslot(k, 7), z_s.at[k, 0, 1], z_r.at[k, 0, 1], dev(dz=7)))
@@ -188,6 +201,12 @@
     def stage_q(k):
         for s in range(1, ZS):
             arrived(hslot(k, s), zd_r.at[k, s - 1])
+
+    def stage_p(k):
+        for way, (near, far, third) in enumerate(((1, 2, 3), (7, 6, 5))):
+            arrived(hslot(k, far), z_r.at[k, 1, way])
+            sends.append(send(hslot(k, far), hslot(k, third), z_s.at[k, 2, way], z_r.at[k, 2, way], dev(dz=near)))
+            sends.append(send(hhalf(k, far, way), hhalf(k, 4, way), z_s.at[k, 3, way], z_r.at[k, 3, way], dev(dz=far)))
 
     def stage_z(k, t):
         arrived(hslot(k, t), z_r.at[k, t - 1, 0])
@@ -202,6 +221,10 @@
             sends.append(send(hhalf(k, 5, 1), hhalf(k, 4, 1), z_s.at[k, 3, 1], z_r.at[k, 3, 1], dev(dz=7)))
 
     def stage_z5(k):
+        if k in PAIRED:
+            for way, (near, third) in enumerate(((1, 3), (7, 5))):
+                arrived(hslot(k, near), z_r.at[k, 0, way])
+                arrived(hslot(k, third), z_r.at[k, 2, way])
         arrived(hhalf(k, 4, 0), z_r.at[k, 3, 0])
         arrived(hhalf(k, 4, 1), z_r.at[k, 3, 1])
 
@@ -353,6 +376,36 @@
 
         accumulate(k)
 
+    def sent_y(k):
+        @pl.when(on_line & (d != 3))
+        def _():
+            bcopy(hidz, k, 0, True).wait_send()
+
+        @pl.when(on_line & (d != 1))
+        def _():
+            bcopy(hidz, k, 1, True).wait_send()
+
+        @pl.when(on_line)
+        def _():
+            bcopy(hidz, k, 0, False).wait_send()
+            bcopy(hidz, k, 1, False).wait_send()
+
+    def sent_e(k):
+        for i in (1, 2, 3):
+            side_copy(k, i).wait_send()
+        for j in range(YS):
+            @pl.when(z != block_of(j))
+            def _():
+                block_copy(k, j).wait_send()
+
+        @pl.when(on_line)
+        def _():
+            line_copy(k).wait_send()
+
+    def flush():
+        while sends:
+            sends.pop().wait_send()
+
     stage_a(0)
     for k, (dx, lo, n, _) in enumerate(CHUNKS):
         if dx > 0:
@@ -362,100 +415,70 @@
             rows[piece_rows(k, y, c), :] = packed[x, lo : lo + n]
 
     stage_b(0)
-    stage_s(0)
     stage_a(1)
     stage_c(0)
     stage_b(1)
+    stage_s(0)
+    stage_a(2)
     stage_d(0)
-    stage_a(2)
     stage_s(1)
-    stage_a(3)
     stage_c(1)
     stage_z(0, 1)
+    stage_b(2)
     stage_d(1)
-    stage_b(2)
-    stage_a(4)
+    stage_a(3)
     stage_z(0, 2)
+    stage_s(2)
+    stage_c(2)
     stage_z(1, 1)
+    stage_z(0, 3)
     stage_b(3)
-    stage_s(2)
-    stage_z(0, 3)
-    stage_c(2)
+    stage_d(2)
+    stage_z5(0)
+    stage_y1(0)
+    stage_e(2)
     stage_s(3)
     stage_z(1, 2)
-    stage_b(4)
-    stage_z5(0)
-    stage_y1(0)
-    stage_d(2)
     stage_c(3)
+    stage_z(2, 1)
     stage_z(1, 3)
-    stage_e(2)
-    stage_s(4)
-    stage_c(4)
+    stage_y2(0)
     stage_d(3)
+    stage_z5(1)
+    stage_f(2)
+    stage_y1(1)
     stage_e(3)
-    stage_z(2, 1)
-    stage_d(4)
+    stage_y2(1)
     stage_z(3, 1)
-    stage_z5(1)
-    stage_y1(1)
+    stage_y3(0)
+    stage_z(2, 2)
     stage_f(3)
-    stage_y2(0)
-    stage_e(4)
-    stage_y2(1)
-    stage_q(4)
-    stage_f(2)
-    stage_y3(0)
+    stage_w(2)
     stage_y3(1)
+    stage_z(2, 3)
+    stage_z(3, 2)
+    stage_y4(0)
+    stage_z5(2)
     stage_w(3)
-    stage_z(2, 2)
-    stage_z(3, 2)
-    stage_f(4)
-    stage_y4(0)
-    stage_w(2)
-    stage_z(2, 3)
+    stage_g(2)
     stage_z(3, 3)
+    flush()
     stage_y4(1)
-    stage_w(4)
-    stage_z5(2)
-    stage_g(2)
     stage_z5(3)
     stage_g(3)
-    stage_g(4)
 
     used = hid[:, ROWS : ROWS + COUNT_ROWS, 0:128].astype(F32)
     count = jnp.sum(used) * (1.0 / (4 * 128))
-    mean_ref[...] = colsum[:, 0:units] / count
+    mean_ref[...] = colsum[0:1, 0:units] / count
     row_mean = gram[:, units : units + 1] / count
     col_mean = colsum[0:1, units:] / count
     cov_ref[...] = gram[:, 0:units] / count - row_mean * col_mean
 
-    for copy in sends:
-        copy.wait_send()
+    flush()
     for k in RELAY:
-        @pl.when(on_line & (d != 3))
-        def _():
-            bcopy(hidz, k, 0, True).wait_send()
-
-        @pl.when(on_line & (d != 1))
-        def _():
-            bcopy(hidz, k, 1, True).wait_send()
-
-        @pl.when(on_line)
-        def _():
-            bcopy(hidz, k, 0, False).wait_send()
-            bcopy(hidz, k, 1, False).wait_send()
+        sent_y(k)
     for k in DIRECT:
-        for i in (1, 2, 3):
-            side_copy(k, i).wait_send()
-        for j in range(YS):
-            @pl.when(z != block_of(j))
-            def _():
-                block_copy(k, j).wait_send()
-
-        @pl.when(on_line)
-        def _():
-            line_copy(k).wait_send()
+        sent_e(k)
 
 
 def local(tokens, routes, slots, gate_weight, up_weight):
@@ -470,11 +493,14 @@
         kernel,
         out_shape=(
             jax.ShapeDtypeStruct((units, units), F32),
-            jax.ShapeDtypeStruct((8, units), F32),
+            jax.ShapeDtypeStruct((1, units), F32),
         ),
-        in_specs=[vmem, vmem, vmem, hbm, hbm],
+        in_specs=[hbm, hbm, hbm, hbm, hbm],
         out_specs=(vmem, vmem),
         scratch_shapes=[
+            pltpu.VMEM(tokens.shape, BF16),
+            pltpu.VMEM(routes.shape[::-1], jnp.int32),
+            pltpu.VMEM(routes.shape[::-1], jnp.int32),
             pltpu.VMEM((XS, CAP, depth + FLAG), BF16),
             pltpu.VMEM((ROWS, depth + FLAG), BF16),
             pltpu.VMEM((depth, units), BF16),
@@ -484,7 +510,7 @@
             pltpu.VMEM((YS - 1, ROWS, units), BF16),
             pltpu.VMEM((units, units + 128), F32),
             pltpu.VMEM((8, 2 * units), F32),
-            dma((2,)), dma((nk,)),
+            dma((5,)), dma((nk,)),
             dma((nk,)), dma((nk,)),
             dma((nk, 2, 2)), dma((nk, 2, 2)),
             dma((nk, 2)), dma((nk, 2)),
@@ -501,7 +527,7 @@
         ),
         name="moments",
     )(tokens, routes.T, slots.T, gate_weight, up_weight)
-    return means[0], cov
+    return means.reshape(units), cov
 
 
 def solution(mesh):

time: 85.5 us -> 80.2 us (0.938)
  the two profiles are of different devices: /device:TPU:17 before, /device:TPU:9 now
where the time goes in v3:
time: 80.2 us; the launch traced here: 79.5 us
  Pallas kernels  75.9 us (95%)
  local copies, waits for them, and re-layouts  2.9 us (4%)
    pallas_call x1, Pallas kernels, local(): pl.pallas_call(kernel, out_shape=(jax.ShapeDtypeStruct((units, units), F3...  75.9 us
    unnamed x2, local copies, waits for them, and re-layouts  2.9 us

profile of v3, /device:TPU:9, one launch (start us, length us, event | category | flops | bytes accessed | tf_op | source)
XLA Modules:
  0.0 79.5 jit_solution(3831051357103006466)
XLA Ops:
  0.6 75.9 %moments.1 = (f32[256,256]{1,0:T(8,128)}, f32[1,256]{1,0:T(1,128)}) custom-call(bf16[128,7168]{1,0:T(8,128)(2,1)} %tok_hbm.1, s32[8,128]{1,0:T(8,128)} %bitcast.3, s32[8,128]{1,0:T(8,128)} %bitcast.4, bf16[7168,256]{1,0:T(8,128)(2,1)} %wg_hbm.1, bf16[7168,256]{1,0:T(8,128)(2,1)} %wu_hbm.1), custom_call_target="tpu_custom_call" | custom-call | tf_op jit(solution)/shard_map/moments/pallas_call | solution.py:492
  76.6 1.2 %copy.9 = f32[256]{0:T(256)} copy(f32[256]{0:T(256)} %bitcast.5) | data formatting | bytes 2048
  77.8 1.7 %copy.10 = f32[256,256]{1,0:T(8,128)} copy(f32[256,256]{1,0:T(8,128)} %get-tuple-element.9) | data formatting | bytes 524288

commit v4 on v3

--- a/solution.py
+++ b/solution.py
@@ -181,12 +181,9 @@
         gate = jnp.dot(lhs, wg[...], preferred_element_type=F32)
         up = jnp.dot(lhs, wu[...], preferred_element_type=F32)
         hid[0, at : at + n, :] = (gate / (1.0 + jnp.exp(-gate)) * up).astype(BF16)
-        if k == last:
-            for r in range(4):
-                part = ROWS // 4
-                used = jnp.sum(rows[r * part : (r + 1) * part, depth:wide].astype(F32), axis=0, keepdims=True)
-                used = jnp.concatenate([used, used], axis=1)
-                hid[0, ROWS + 4 * r : ROWS + 4 * (r + 1), :] = jnp.broadcast_to(used, (4, units)).astype(BF16)
+        used = jnp.sum(rows[at : at + n, depth:wide].astype(F32), axis=0, keepdims=True)
+        used = jnp.concatenate([used, used], axis=1)
+        hid[0, ROWS + 4 * k : ROWS + 4 * (k + 1), :] = jnp.broadcast_to(used, (4, units)).astype(BF16)
         if k in STRAIGHT:
             for s in (4, 3, 5, 2, 6, 1, 7):
                 sends.append(send(hslot(k, 0), hslot(k, s), zd_s.at[k, s - 1], zd_r.at[k, s - 1], dev(dz=s)))
@@ -353,7 +350,7 @@
             block_copy(k, j).start()
 
     def stage_e(k):
-        for i in (1, 3, 2):
+        for i in (2, 1, 3):
             side_copy(k, i).start()
         pass_on(k, 0)
 
@@ -444,25 +441,25 @@
     stage_z(1, 3)
     stage_y2(0)
     stage_d(3)
+    stage_e(3)
     stage_z5(1)
+    stage_y1(1)
     stage_f(2)
-    stage_y1(1)
-    stage_e(3)
-    stage_y2(1)
     stage_z(3, 1)
-    stage_y3(0)
     stage_z(2, 2)
     stage_f(3)
+    stage_y2(1)
+    stage_y3(0)
     stage_w(2)
+    stage_z(3, 2)
     stage_y3(1)
     stage_z(2, 3)
-    stage_z(3, 2)
     stage_y4(0)
     stage_z5(2)
+    stage_z(3, 3)
+    stage_g(2)
+    flush()
     stage_w(3)
-    stage_g(2)
-    stage_z(3, 3)
-    flush()
     stage_y4(1)
     stage_z5(3)
     stage_g(3)

time: 80.2 us -> 80.3 us (level)
  the two profiles are of different devices: /device:TPU:9 before, /device:TPU:29 now
where the time goes in v4:
time: 80.3 us; the launch traced here: 80.2 us
  Pallas kernels  76.6 us (95%)
  local copies, waits for them, and re-layouts  2.9 us (4%)
    pallas_call x1, Pallas kernels, local(): pl.pallas_call(kernel, out_shape=(jax.ShapeDtypeStruct((units, units), F3...  76.6 us
    unnamed x2, local copies, waits for them, and re-layouts  2.9 us

profile of v4, /device:TPU:29, one launch (start us, length us, event | category | flops | bytes accessed | tf_op | source)
XLA Modules:
  0.0 80.2 jit_solution(3320653427134544695)
XLA Ops:
  0.6 76.6 %moments.1 = (f32[256,256]{1,0:T(8,128)}, f32[1,256]{1,0:T(1,128)}) custom-call(bf16[128,7168]{1,0:T(8,128)(2,1)} %tok_hbm.1, s32[8,128]{1,0:T(8,128)} %bitcast.3, s32[8,128]{1,0:T(8,128)} %bitcast.4, bf16[7168,256]{1,0:T(8,128)(2,1)} %wg_hbm.1, bf16[7168,256]{1,0:T(8,128)(2,1)} %wu_hbm.1), custom_call_target="tpu_custom_call" | custom-call | tf_op jit(solution)/shard_map/moments/pallas_call | solution.py:489
  77.3 1.2 %copy.9 = f32[256]{0:T(256)} copy(f32[256]{0:T(256)} %bitcast.5) | data formatting | bytes 2048
  78.5 1.7 %copy.10 = f32[256,256]{1,0:T(8,128)} copy(f32[256,256]{1,0:T(8,128)} %get-tuple-element.9) | data formatting | bytes 524288
